TPU v7x, 256 devices: a whole 4x4x8 slice. The times are simulated.
256 devices in a mesh: chan: 8 (over x, core), ctx: 32 (over z, y).
Axes of the slice: x: 4, y: 4, z: 8, core: 2. Of those that a mesh axis runs over, the one named last changes fastest.
Arguments:
- queries: bfloat16 [4096, 8192], P('ctx', 'chan'), may hold values from -6 to 6
- keys: bfloat16 [4096, 8192], P('ctx', 'chan'), may hold values from -6 to 6
- values: bfloat16 [4096, 8192], P('ctx', 'chan'), may hold values from -6 to 6
- filters: bfloat16 [4, 4096], P(None, 'ctx'), may hold values from -0.09375 to 0.09375
- cotangent: bfloat16 [4096, 8192], P('ctx', 'chan'), may hold values from -6 to 6
Outputs:
- output: bfloat16 [4096, 8192], P('ctx', 'chan')
- query_grad: bfloat16 [4096, 8192], P('ctx', 'chan')
- key_grad: bfloat16 [4096, 8192], P('ctx', 'chan')
- value_grad: bfloat16 [4096, 8192], P('ctx', 'chan')
- filter_grad: float32 [4, 4096], P(None, 'ctx')
All inputs are finite; a program needn't handle non-finite values.
Results may differ from a plain program's by a relative error of at most 0.015.
Values may be sent and summed in bfloat16 or wider, within the bound.
A program may use at most 64 MiB of HBM per device.

v0:
```python
import jax
import jax.numpy as jnp
from jax import lax
from jax.sharding import PartitionSpec as P

D = 8192
NFILT = 4


def toeplitz(padded, base, height, breadth):
    middle = padded.shape[1] // 2
    span = height + breadth - 1
    window = lax.dynamic_slice_in_dim(padded, middle + base - breadth + 1, span, 1)
    flipped = window[:, ::-1]
    tiled = jnp.tile(flipped, (1, height + 1))
    flat = tiled[:, height - 1 : height - 1 + height * (span - 1)]
    return flat.reshape(padded.shape[0], height, span - 1)[:, :, :breadth]


def diagonal_sums(product):
    nfil, height, breadth = product.shape
    stride = height + breadth
    flipped = product[:, :, ::-1]
    padded = jnp.pad(flipped, ((0, 0), (0, 0), (0, height)))
    flat = padded.reshape(nfil, height * stride)[:, : height * (stride - 1)]
    return jnp.sum(flat.reshape(nfil, height, stride - 1), axis=1)


def add_lags(lag_acc, sums, first_lag):
    middle = lag_acc.shape[1] // 2
    where = middle + first_lag
    current = lax.dynamic_slice_in_dim(lag_acc, where, sums.shape[1], 1)
    return lax.dynamic_update_slice_in_dim(lag_acc, current + sums, where, 1)


def in_blocks(block_fn, carry, piece, rows):
    count = piece.shape[0]
    size = rows * max(1, 512 // rows)
    parts = piece.reshape((count // size, size) + piece.shape[1:])
    offsets = jnp.arange(count // size, dtype=jnp.int32) * size

    def visit(state, item):
        block, offset = item
        return (block_fn(state, block, offset), None)

    result, unused = lax.scan(visit, carry, (parts, offsets))
    return result


def shards(queries, keys, values, filters, cotangent):
    rows, width = queries.shape
    nfil = filters.shape[0]
    narrow = width // nfil
    gated = (keys.astype(jnp.float32) * values.astype(jnp.float32)).astype(jnp.bfloat16)
    back = (cotangent.astype(jnp.float32) * queries.astype(jnp.float32)).astype(jnp.bfloat16)
    taps = lax.all_gather(filters, "ctx", axis=1, tiled=True)
    total = taps.shape[1]
    padded = jnp.concatenate([jnp.zeros_like(taps), taps], axis=1)
    lag_start = jnp.zeros((nfil, 2 * total), jnp.float32)
    first = lax.axis_index("ctx") * rows
    back_cols = back.reshape(rows, narrow, nfil)

    def forward_block(carry, piece, start):
        count = piece.shape[0]

        def forward_work(state):
            mixed_acc, lag_acc = state
            tile = toeplitz(padded, first - start, rows, count)
            columns = piece.reshape(count, narrow, nfil)
            mixed_acc = mixed_acc + jnp.einsum(
                "fst,tcf->scf", tile, columns, preferred_element_type=jnp.float32
            )
            product = jnp.einsum(
                "scf,tcf->fst", back_cols, columns, preferred_element_type=jnp.float32
            )
            lag_acc = add_lags(lag_acc, diagonal_sums(product), first - start - count + 1)
            return (mixed_acc, lag_acc)

        return lax.cond(start < first + rows, forward_work, lambda state: state, carry)

    empty = jnp.zeros((rows, narrow, nfil), jnp.float32)
    mixed_acc, lag_part = in_blocks(
        forward_block, (empty, lag_start), lax.all_gather(gated, "ctx", axis=0, tiled=True), rows
    )

    def backward_block(grad_acc, piece, start):
        count = piece.shape[0]

        def backward_work(state):
            tile = toeplitz(padded, start - first, count, rows)
            columns = piece.reshape(count, narrow, nfil)
            return state + jnp.einsum(
                "fst,scf->tcf", tile, columns, preferred_element_type=jnp.float32
            )

        return lax.cond(start + count > first, backward_work, lambda state: state, grad_acc)

    grad_acc = in_blocks(
        backward_block, empty, lax.all_gather(back, "ctx", axis=0, tiled=True), rows
    )
    mixed = mixed_acc.reshape(rows, width)
    gated_grad = grad_acc.reshape(rows, width)
    lag_share = lax.psum_scatter(
        lag_part[:, total:].astype(jnp.bfloat16), "ctx", scatter_dimension=1, tiled=True
    ).astype(jnp.float32)
    lag_total = lax.psum(lag_share, "chan")
    scale = (total * (D // NFILT)) ** (-0.5)
    filter_grad = lag_total * scale
    output = (queries.astype(jnp.float32) * mixed).astype(jnp.bfloat16)
    query_grad = (cotangent.astype(jnp.float32) * mixed).astype(jnp.bfloat16)
    key_grad = (gated_grad * values.astype(jnp.float32)).astype(jnp.bfloat16)
    value_grad = (gated_grad * keys.astype(jnp.float32)).astype(jnp.bfloat16)
    return (output, query_grad, key_grad, value_grad, filter_grad)


def solution(mesh):
    placed = (
        P("ctx", "chan"),
        P("ctx", "chan"),
        P("ctx", "chan"),
        P(None, "ctx"),
        P("ctx", "chan"),
    )
    return jax.shard_map(
        shards,
        mesh=mesh,
        in_specs=placed,
        out_specs=(
            P("ctx", "chan"),
            P("ctx", "chan"),
            P("ctx", "chan"),
            P("ctx", "chan"),
            P(None, "ctx"),
        ),
        check_vma=False,
    )
```

profile of v0, /device:TPU:1, one launch (start us, length us, event | category | flops | bytes accessed | tf_op | source)
XLA Modules:
  0.0 846.8 jit_solution(6806432111096197766)
XLA Ops:
  12.5 38.3 %all_gather.9 = bf16[4,4096]{1,0:T(4,128)(2,1)S(1)} all-gather(bf16[4,128]{1,0:T(4,128)(2,1)S(1)} %copy-done.7), channel_id=1, replica_groups=mesh['chan'=8,'ctx'=32] {'ctx'}, dimensions={1}, use_global_device_ids=true | all-gather | bytes 33792 | tf_op jit(solution)/shard_map/all_gather | solution.py:56
  50.8 65.4 %all-gather.5.cloned.1.call-done = bf16[4096,1024]{0,1:T(8,128)(2,1)} async-done(((bf16[128,1024]{0,1:T(8,128)(2,1)}), bf16[4096,1024]{0,1:T(8,128)(2,1)}) %all-gather.5.cloned.1.call-update) | async-done | bytes 8388624 | tf_op jit(solution)/shard_map/all_gather | solution.py:99
  116.2 7.4 copy.60
  123.7 238.9 %while.27 = (s32[]{:T(128)}, f32[128,256,4]{1,0,2:T(8,128)S(1)}, s32[8]{0:T(128)S(1)}, s32[]{:T(128)}, bf16[4,8192]{1,0:T(4,128)(2,1)S(1)}, /*index=5*/bf16[8,512,1024]{1,2,0:T(8,128)(2,1)}, s32[]{:T(128)}, s32[]{:T(128)}) while((s32[]{:T(128)}, f32[128,256,4]{1,0,2:T(8,128)S(1)}, s32[8]{0:T(128)S(1)}, s32[]{:T(128)}, ...), condition=%wide.region_8.9_spmd, body=%wide.region_5.8_spmd.sunk | while | flops 134348800 | bytes 35643552 | solution.py:46
  125.0 28.5 %conditional.5 = (f32[128,256,4]{1,0,2:T(8,128)S(1)}) conditional(s32[]{:T(128)} %convert_element_type.91, f32[128,256,4]{1,0,2:T(8,128)S(1)} %get-tuple-element.399, (s32[]{:T(128)}, s32[]{:T(128)}, bf16[4,8192]{1,0:T(4,128)(2,1)S(1)}, bf16[8,512,1024]{1,2,0:T(8,128)(2,1)}, s32[]{:T(128)}, /*index=5*/f32[128,256,4]{1,0,2:T(8,128)S(1)}) %tuple.73), branch_computations={%region_6.6_spmd, %region_7.7_spmd} | conditional | flops 134348800 | bytes 35643384 | solution.py:96
  126.6 6.1 reshape.68
  132.7 5.1 tile.14
  137.8 3.0 slice.28
  140.8 2.7 reshape.70
  143.5 6.8 reshape.54
  151.9 1.6 fusion.2
  154.9 28.5 %conditional.5 = (f32[128,256,4]{1,0,2:T(8,128)S(1)}) conditional(s32[]{:T(128)} %convert_element_type.91, f32[128,256,4]{1,0,2:T(8,128)S(1)} %get-tuple-element.399, (s32[]{:T(128)}, s32[]{:T(128)}, bf16[4,8192]{1,0:T(4,128)(2,1)S(1)}, bf16[8,512,1024]{1,2,0:T(8,128)(2,1)}, s32[]{:T(128)}, /*index=5*/f32[128,256,4]{1,0,2:T(8,128)S(1)}) %tuple.73), branch_computations={%region_6.6_spmd, %region_7.7_spmd} | conditional | flops 134348800 | bytes 35643384 | solution.py:96
  156.5 6.1 reshape.68
  162.6 5.1 tile.14
  167.7 3.0 slice.28
  170.7 2.7 reshape.70
  173.4 6.8 reshape.54
  184.8 28.5 %conditional.5 = (f32[128,256,4]{1,0,2:T(8,128)S(1)}) conditional(s32[]{:T(128)} %convert_element_type.91, f32[128,256,4]{1,0,2:T(8,128)S(1)} %get-tuple-element.399, (s32[]{:T(128)}, s32[]{:T(128)}, bf16[4,8192]{1,0:T(4,128)(2,1)S(1)}, bf16[8,512,1024]{1,2,0:T(8,128)(2,1)}, s32[]{:T(128)}, /*index=5*/f32[128,256,4]{1,0,2:T(8,128)S(1)}) %tuple.73), branch_computations={%region_6.6_spmd, %region_7.7_spmd} | conditional | flops 134348800 | bytes 35643384 | solution.py:96
  186.3 6.1 reshape.68
  192.4 5.1 tile.14
  197.5 3.0 slice.28
  200.5 2.7 reshape.70
  203.2 6.8 reshape.54
  214.6 28.5 %conditional.5 = (f32[128,256,4]{1,0,2:T(8,128)S(1)}) conditional(s32[]{:T(128)} %convert_element_type.91, f32[128,256,4]{1,0,2:T(8,128)S(1)} %get-tuple-element.399, (s32[]{:T(128)}, s32[]{:T(128)}, bf16[4,8192]{1,0:T(4,128)(2,1)S(1)}, bf16[8,512,1024]{1,2,0:T(8,128)(2,1)}, s32[]{:T(128)}, /*index=5*/f32[128,256,4]{1,0,2:T(8,128)S(1)}) %tuple.73), branch_computations={%region_6.6_spmd, %region_7.7_spmd} | conditional | flops 134348800 | bytes 35643384 | solution.py:96
  216.2 6.1 reshape.68
  222.3 5.1 tile.14
  227.4 3.0 slice.28
  230.4 2.7 reshape.70
  233.1 6.8 reshape.54
  244.5 28.5 %conditional.5 = (f32[128,256,4]{1,0,2:T(8,128)S(1)}) conditional(s32[]{:T(128)} %convert_element_type.91, f32[128,256,4]{1,0,2:T(8,128)S(1)} %get-tuple-element.399, (s32[]{:T(128)}, s32[]{:T(128)}, bf16[4,8192]{1,0:T(4,128)(2,1)S(1)}, bf16[8,512,1024]{1,2,0:T(8,128)(2,1)}, s32[]{:T(128)}, /*index=5*/f32[128,256,4]{1,0,2:T(8,128)S(1)}) %tuple.73), branch_computations={%region_6.6_spmd, %region_7.7_spmd} | conditional | flops 134348800 | bytes 35643384 | solution.py:96
  246.1 6.1 reshape.68
  252.1 5.1 tile.14
  257.3 3.0 slice.28
  260.2 2.7 reshape.70
  263.0 6.8 reshape.54
  271.4 1.6 fusion.2
  274.4 28.5 %conditional.5 = (f32[128,256,4]{1,0,2:T(8,128)S(1)}) conditional(s32[]{:T(128)} %convert_element_type.91, f32[128,256,4]{1,0,2:T(8,128)S(1)} %get-tuple-element.399, (s32[]{:T(128)}, s32[]{:T(128)}, bf16[4,8192]{1,0:T(4,128)(2,1)S(1)}, bf16[8,512,1024]{1,2,0:T(8,128)(2,1)}, s32[]{:T(128)}, /*index=5*/f32[128,256,4]{1,0,2:T(8,128)S(1)}) %tuple.73), branch_computations={%region_6.6_spmd, %region_7.7_spmd} | conditional | flops 134348800 | bytes 35643384 | solution.py:96
  275.9 6.1 reshape.68
  282.0 5.1 tile.14
  287.1 3.0 slice.28
  290.1 2.7 reshape.70
  292.8 6.8 reshape.54
  304.2 28.5 %conditional.5 = (f32[128,256,4]{1,0,2:T(8,128)S(1)}) conditional(s32[]{:T(128)} %convert_element_type.91, f32[128,256,4]{1,0,2:T(8,128)S(1)} %get-tuple-element.399, (s32[]{:T(128)}, s32[]{:T(128)}, bf16[4,8192]{1,0:T(4,128)(2,1)S(1)}, bf16[8,512,1024]{1,2,0:T(8,128)(2,1)}, s32[]{:T(128)}, /*index=5*/f32[128,256,4]{1,0,2:T(8,128)S(1)}) %tuple.73), branch_computations={%region_6.6_spmd, %region_7.7_spmd} | conditional | flops 134348800 | bytes 35643384 | solution.py:96
  305.8 6.1 reshape.68
  311.9 5.1 tile.14
  317.0 3.0 slice.28
  320.0 2.7 reshape.70
  322.7 6.8 reshape.54
  331.1 1.6 fusion.2
  334.1 28.5 %conditional.5 = (f32[128,256,4]{1,0,2:T(8,128)S(1)}) conditional(s32[]{:T(128)} %convert_element_type.91, f32[128,256,4]{1,0,2:T(8,128)S(1)} %get-tuple-element.399, (s32[]{:T(128)}, s32[]{:T(128)}, bf16[4,8192]{1,0:T(4,128)(2,1)S(1)}, bf16[8,512,1024]{1,2,0:T(8,128)(2,1)}, s32[]{:T(128)}, /*index=5*/f32[128,256,4]{1,0,2:T(8,128)S(1)}) %tuple.73), branch_computations={%region_6.6_spmd, %region_7.7_spmd} | conditional | flops 134348800 | bytes 35643384 | solution.py:96
  335.6 6.1 reshape.68
  341.7 5.1 tile.14
  346.9 3.0 slice.28
  349.8 2.7 reshape.70
  352.6 6.8 reshape.54
  362.9 1.8 fusion.6
  366.8 96.9 %all-gather.3.cloned.1.call-done = bf16[4096,1024]{0,1:T(8,128)(2,1)} async-done(((bf16[128,1024]{0,1:T(8,128)(2,1)}), bf16[4096,1024]{0,1:T(8,128)(2,1)}) %all-gather.3.cloned.1.call-update) | async-done | bytes 8388624 | tf_op jit(solution)/shard_map/all_gather | solution.py:83
  463.7 7.4 copy.61
  471.9 26.2 %while.26 = (s32[]{:T(128)}, f32[128,256,4]{1,0,2:T(8,128)}, f32[4,8192]{1,0:T(4,128)S(1)}, s32[8]{0:T(128)S(1)}, s32[]{:T(128)}, /*index=5*/s32[]{:T(128)}, bf1...) while((s32[]{:T(128)}, f32[128,256,4]{1,0,2:T(8,128)}, ...), condition=%wide.region_4.5_spmd, body=%wide.region_0.4_spmd.sunk | while | flops 268893696 | bytes 31679636 | solution.py:46
  473.2 16.0 %conditional.4 = ((f32[128,256,4]{1,0,2:T(8,128)}, f32[4,8192]{1,0:T(4,128)S(1)})) conditional(s32[]{:T(128)} %convert_element_type.90, (f32[128,256,4]{1,0,2:T(8,128)}, f32[4,8192]{1,0:T(4,128)S(1)}) %tuple.70, (s32[]{:T(128)}, s32[]{:T(128)}, bf16[4,8192]{1,0:T(4,128)(2,1)}, bf16[8,512,1024]{1,2,0:T(8,128)(2,1)}, s32[]{:T(128)}, ...), branch_computations={%region_1.1_spmd, %region_2.3_spmd} | conditional | flops 268893696 | bytes 31679430 | solution.py:79
  479.7 2.9 reshape.53
  487.0 2.1 fusion
  502.8 318.5 %reduce-scatter.4.cloned.1.call-done = bf16[128,4]{1,0:T(8,128)(2,1)} async-done(((bf16[4096,4]{1,0:T(8,128)(2,1)}), bf16[128,4]{1,0:T(8,128)(2,1)}) %reduce-scatter.4.cloned.1.call-update) | async-done | bytes 1040
  822.1 17.6 %psum.7 = f32[4,128]{1,0:T(4,128)S(1)} all-reduce(bf16[4,128]{1,0:T(4,128)(2,1)S(1)} %copy.50), channel_id=1, replica_groups=mesh['chan'=8,'ctx'=32] {'chan'}, use_global_device_ids=true, to_apply=%region_10.11 | all-reduce | flops 512 | bytes 3072 | tf_op jit(solution)/shard_map/psum | solution.py:106
  (139 shorter events, 61.9 us)
Async XLA Ops:
  7.2 4.5 copy-start.5
  7.2 5.3 copy-start.7
  7.2 109.0 %all-gather.5.cloned.1.call-start = ((), (), s32[]{:S(2)}) async-start(), calls=%async_computation.2 | async-start | bytes 8650752 | tf_op jit(solution)/shard_map/all_gather | solution.py:99
  8.4 115.2 %copy-start.1 = (bf16[128,1024]{0,1:T(8,128)(2,1)}, bf16[128,1024]{0,1:T(8,128)(2,1)S(1)}, u32[]{:S(2)}) copy-start(bf16[128,1024]{0,1:T(8,128)(2,1)S(1)} %copy.36) | copy-start | bytes 786436
  9.6 114.0 %copy-start.3 = (bf16[128,1024]{0,1:T(8,128)(2,1)}, bf16[128,1024]{0,1:T(8,128)(2,1)S(1)}, u32[]{:S(2)}) copy-start(bf16[128,1024]{0,1:T(8,128)(2,1)S(1)} %copy.39) | copy-start | bytes 786436
  10.4 453.2 %all-gather.3.cloned.1.call-start = ((), (), s32[]{:S(2)}) async-start(), calls=%async_computation.1 | async-start | bytes 8650752 | tf_op jit(solution)/shard_map/all_gather | solution.py:83
  362.6 108.5 %copy-start.6 = (bf16[4,8192]{1,0:T(4,128)(2,1)}, bf16[4,8192]{1,0:T(4,128)(2,1)S(1)}, u32[]{:S(2)}) copy-start(bf16[4,8192]{1,0:T(4,128)(2,1)S(1)} %get-tuple-element.458) | copy-start | bytes 196612
  362.6 2.3 copy-start
  364.7 456.6 %reduce-scatter.4.cloned.1.call-start = ((), (), s32[]{:S(2)}) async-start(), calls=%async_computation.3 | async-start | bytes 1081344
  498.1 2.8 copy-start.2
  498.1 2.8 copy-start.4
Sparse Core Ops, SparseCore 0:
  11.1 105.0 all-gather.4
  364.8 98.8 all-gather.2
  501.1 320.1 reduce-scatter.3
where the time goes:
time: 849 us; the launch traced here: 847 us
  waiting for transfers between devices  481 us (57%)
  local copies, waits for them, and re-layouts  259 us (31%)
  blocking collectives  56 us (7%)
  loops' own time  17.9 us (2%)
  matrix products  15.2 us (2%)
  between operations  14 us (2%)
    unnamed x4, waiting for transfers between devices  319 us
    all_gather x1, waiting for transfers between devices, shards(): lax.all_gather(gated, 'ctx', axis=0, tiled=True)  96.9 us
    cond x37, local copies, waits for them, and re-layouts  76.6 us
    all_gather x1, waiting for transfers between devices, shards(): lax.all_gather(back, 'ctx', axis=0, tiled=True)  65.4 us
    reshape x9, local copies, waits for them, and re-layouts, toeplitz(): return flat.reshape(padded.shape[0], height, span - 1)[:, :, :breadth]  56.2 us
    another operation x18, local copies, waits for them, and re-layouts, toeplitz(): tiled = jnp.tile(flipped, (1, height + 1))  43.2 us
    all_gather x1, blocking collectives, shards(): taps = lax.all_gather(filters, 'ctx', axis=1, tiled=True)  38.3 us
    slice x9, local copies, waits for them, and re-layouts, toeplitz(): flat = tiled[:, height - 1:height - 1 + height * (span - 1)]  24.4 us
  transfers between devices with their start and end apart: 3, of which 3 were waited for; matrix products, arithmetic and copies ran while one was open for 1% of the time, Pallas kernels for 0%

commit v1 on v0

v1 whole, which is shorter than its diff:
```python
import functools

import jax
import jax.numpy as jnp
from jax import lax
from jax.experimental import pallas as pl
from jax.experimental.pallas import tpu as pltpu
from jax.sharding import PartitionSpec as P

NFILT = 4
PLANES = 8
RING = 4
CTX = PLANES * RING
ROWS = 128
BLOCK = 256
NBLOCK = 16
SHARE = 32
GROUPS = 4
MESH = pl.DeviceIdType.MESH
F32 = jnp.float32
BF16 = jnp.bfloat16


def dot(a, b, ca, cb):
    return lax.dot_general(a, b, (((ca,), (cb,)), ((), ())), preferred_element_type=F32)


def kernel(nchan, scale,
           q_ref, k_ref, v_ref, taps_ref, c_ref,
           out_ref, qg_ref, kg_ref, vg_ref, fg_ref,
           sg, sb, rg, rb, om, og, bm, bg, ts, tr, toep, acc, gt_t, prod, fa, ra, sbuf, rf,
           t_ss, t_rs, g_ss, g_rs, b_ss, b_rs, m_ss, m_rs, o_ss, o_rs, a_ss, a_rs, f_ss, f_rs):
    ch = lax.axis_index("chan")
    me = lax.axis_index("ctx")
    z = lax.div(me, RING)
    y = lax.rem(me, RING)

    def peer(step):
        n = lax.div(step, RING)
        half = lax.div(n + 1, 2)
        dz = lax.rem(PLANES // 2 + PLANES + (1 - 2 * lax.rem(n, 2)) * half, PLANES)
        dy = lax.rem(step, RING)
        return lax.rem(z + dz, PLANES) * RING + lax.rem(y + dy, RING)

    def each_peer(fn):
        def body(step, carry):
            fn(peer(step))
            return carry
        lax.fori_loop(0, CTX - RING, body, 0)
        lax.fori_loop(CTX - RING + 1, CTX, body, 0)

    def each_plane_peer(fn):
        def body(step, carry):
            p = lax.rem(ch + lax.div(step, RING), nchan)
            fn(p, lax.rem(y + lax.rem(step, RING), RING))
            return carry
        lax.fori_loop(1, nchan * RING, body, 0)

    barrier = pltpu.get_barrier_semaphore()

    def greet(i):
        pl.semaphore_signal(barrier, inc=1, device_id=(ch, i), device_id_type=MESH)

    each_peer(greet)

    def greet_plane(step, carry):
        p = lax.rem(ch + lax.div(step, RING), nchan)
        pl.semaphore_signal(barrier, inc=1, device_id=(p, z * RING + lax.rem(step, RING)),
                            device_id_type=MESH)
        return carry

    lax.fori_loop(RING, nchan * RING, greet_plane, 0)

    row = lax.broadcasted_iota(jnp.int32, (128, 128), 0)
    lane = lax.broadcasted_iota(jnp.int32, (128, 128), 1)
    order = (lane == NFILT * (row % SHARE) + row // SHARE).astype(BF16)

    for f in range(NFILT):
        ts[f] = taps_ref[f:f + 1, :].astype(F32)
    for g in range(PLANES):
        at = slice(g * 128, (g + 1) * 128)
        gated = (k_ref[:, at].astype(F32) * v_ref[:, at].astype(F32)).astype(BF16)
        sg[at, :] = dot(order, gated, 1, 1).astype(BF16)
        back = (c_ref[:, at].astype(F32) * q_ref[:, at].astype(F32)).astype(BF16)
        sb[at, :] = dot(order, back, 1, 1).astype(BF16)

    pl.semaphore_wait(barrier, CTX - 1 + (nchan - 1) * RING)

    def chunk(i):
        return pl.ds(pl.multiple_of(i * SHARE, SHARE), SHARE)

    def place(i):
        return (pl.ds(pl.multiple_of(lax.div(i, 2) * SHARE, SHARE), SHARE),
                pl.ds(pl.multiple_of(lax.rem(i, 2) * 128, 128), 128))

    def copy(src, dst, ss, rs, i):
        return pltpu.make_async_remote_copy(src_ref=src, dst_ref=dst, send_sem=ss, recv_sem=rs,
                                            device_id=(ch, i), device_id_type=MESH)

    def taps_copy(i, src, slot):
        return copy(ts.at[pl.ds(lax.rem(i, RING), 1)], tr.at[pl.ds(src, 1)], t_ss.at[i], t_rs.at[slot], i)

    def in_copy(send, recv, ss, rs):
        def make(i, src, slot):
            r, l = place(src)
            return copy(send.at[chunk(i), :], recv.at[r, l], ss.at[i], rs.at[slot], i)
        return make

    def out_copy(send, recv, ss, rs):
        def make(i, src, slot):
            r, l = place(i)
            return copy(send.at[r, l], recv.at[chunk(src), :], ss.at[i], rs.at[slot], i)
        return make

    g_copy = in_copy(sg, rg, g_ss, g_rs)
    b_copy = in_copy(sb, rb, b_ss, b_rs)
    m_copy = out_copy(om, bm, m_ss, m_rs)
    o_copy = out_copy(og, bg, o_ss, o_rs)

    def send_all(make):
        each_peer(lambda i: make(i, me, me).start())

    def recv_all(make):
        each_peer(lambda i: make(i, i, i).wait_recv())

    def sent_all(make):
        each_peer(lambda i: make(i, me, me).wait_send())

    send_all(taps_copy)
    send_all(g_copy)
    send_all(b_copy)

    pad = GROUPS * SHARE
    my_rows, my_lanes = place(me)
    tr[pl.ds(me, 1)] = ts[pl.ds(y, 1)]
    rg[my_rows, my_lanes] = sg[chunk(me), :]
    rb[my_rows, my_lanes] = sb[chunk(me), :]
    rb[NBLOCK * SHARE:NBLOCK * SHARE + pad, :] = jnp.zeros((pad, BLOCK), BF16)

    recv_all(taps_copy)
    sub = lax.broadcasted_iota(jnp.int32, (BLOCK, BLOCK), 0)
    col = lax.broadcasted_iota(jnp.int32, (BLOCK, BLOCK), 1)

    def build(d, carry):
        this = jnp.concatenate([tr[2 * d], tr[2 * d + 1]], axis=1)
        low = lax.max(d - 1, 0)
        last = jnp.concatenate([tr[2 * low], tr[2 * low + 1]], axis=1)
        last = last * (d > 0).astype(F32)
        picked = jnp.where(sub + col < BLOCK, jnp.broadcast_to(this, (BLOCK, BLOCK)),
                           jnp.broadcast_to(last, (BLOCK, BLOCK)))
        toep[d] = pltpu.roll(picked, 0, 1, stride=1, stride_axis=0).astype(BF16)
        return carry

    lax.fori_loop(0, NBLOCK, build, 0)

    full = NBLOCK * SHARE
    recv_all(g_copy)
    for d in range(NBLOCK):
        part = dot(rg[0:full - SHARE * d, :], toep[d], 1, 0)
        if d == 0:
            acc[...] = part
        else:
            acc[SHARE * d:full, :] += part
    om[...] = acc[...].astype(BF16)
    send_all(m_copy)
    bm[chunk(me), :] = om[my_rows, my_lanes]

    recv_all(b_copy)
    for d in range(NBLOCK):
        part = dot(rb[SHARE * d:full, :], toep[d], 1, 1)
        if d == 0:
            acc[...] = part
        else:
            acc[0:full - SHARE * d, :] += part
    og[...] = acc[...].astype(BF16)
    send_all(o_copy)
    bg[chunk(me), :] = og[my_rows, my_lanes]

    flip = (sub + col == BLOCK - 1).astype(BF16)
    gt_t[...] = dot(flip, rg[...], 1, 1).astype(BF16)
    for group in range(NBLOCK // GROUPS):
        depth = full - group * GROUPS * SHARE
        for s in range(GROUPS):
            d = group * GROUPS + s
            prod[d] = dot(gt_t[:, 0:depth], rb[SHARE * d:SHARE * d + depth, :], 1, 0)
    prod[NBLOCK] = jnp.zeros((BLOCK, BLOCK), F32)

    def lag_sums(plane, carry):
        for e in range(2):
            d = 2 * plane + e
            both = jnp.where(col + sub >= BLOCK - 1, prod[d], prod[d + 1])
            sums = jnp.sum(pltpu.roll(both, 1, 1, stride=1, stride_axis=0), axis=0, keepdims=True)
            fa[RING * plane + 2 * e] = sums[:, 0:128]
            fa[RING * plane + 2 * e + 1] = sums[:, 128:256]
        return carry

    lax.fori_loop(0, PLANES, lag_sums, 0)

    def a_copy(p, src, slot):
        return copy(fa.at[pl.ds(RING * p, RING)], ra.at[src], a_ss.at[p], a_rs.at[slot], RING * p + y)

    def planes(fn):
        def body(step, carry):
            fn(lax.rem(z + step, PLANES))
            return carry
        lax.fori_loop(1, PLANES, body, 0)

    planes(lambda p: a_copy(p, z, z).start())
    ra[z] = fa[pl.ds(RING * z, RING)]

    recv_all(m_copy)
    for g in range(PLANES):
        at = slice(g * 128, (g + 1) * 128)
        mixed = dot(bm[at, :], order, 0, 0)
        out_ref[:, at] = (q_ref[:, at].astype(F32) * mixed).astype(BF16)
        qg_ref[:, at] = (c_ref[:, at].astype(F32) * mixed).astype(BF16)

    planes(lambda p: a_copy(p, p, p).wait_recv())
    total = ra[0]
    for p in range(1, PLANES):
        total = total + ra[p]
    sbuf[...] = total

    def f_copy(p, r, srcp, srcf):
        slot = srcp * RING + srcf
        return pltpu.make_async_remote_copy(
            src_ref=sbuf.at[pl.ds(r, 1)], dst_ref=rf.at[pl.ds(slot, 1)],
            send_sem=f_ss.at[p * RING + r], recv_sem=f_rs.at[slot],
            device_id=(p, z * RING + r), device_id_type=MESH)

    each_plane_peer(lambda p, r: f_copy(p, r, ch, y).start())
    rf[pl.ds(ch * RING + y, 1)] = sbuf[pl.ds(y, 1)]

    recv_all(o_copy)
    for g in range(PLANES):
        at = slice(g * 128, (g + 1) * 128)
        grad = dot(bg[at, :], order, 0, 0)
        kg_ref[:, at] = (grad * v_ref[:, at].astype(F32)).astype(BF16)
        vg_ref[:, at] = (grad * k_ref[:, at].astype(F32)).astype(BF16)

    each_plane_peer(lambda p, r: f_copy(p, r, p, r).wait_recv())
    for f in range(NFILT):
        total = rf[f]
        for p in range(1, nchan):
            total = total + rf[p * RING + f]
        fg_ref[f:f + 1, :] = total * scale

    sent_all(taps_copy)
    sent_all(g_copy)
    sent_all(b_copy)
    sent_all(m_copy)
    sent_all(o_copy)
    planes(lambda p: a_copy(p, z, z).wait_send())
    each_plane_peer(lambda p, r: f_copy(p, r, ch, y).wait_send())


def shards(nchan, queries, keys, values, filters, cotangent):
    rows, width = queries.shape
    tokens = rows * CTX
    scale = (tokens * (nchan * width // NFILT)) ** (-0.5)
    vmem = pl.BlockSpec(memory_space=pltpu.VMEM)
    dma = pltpu.SemaphoreType.DMA
    full = NBLOCK * SHARE
    act = jax.ShapeDtypeStruct((rows, width), BF16)
    return pl.pallas_call(
        functools.partial(kernel, nchan, scale),
        out_shape=(act, act, act, act, jax.ShapeDtypeStruct((NFILT, rows), F32)),
        in_specs=[vmem] * 5,
        out_specs=[vmem] * 5,
        scratch_shapes=[
            pltpu.VMEM((width, rows), BF16),
            pltpu.VMEM((width, rows), BF16),
            pltpu.VMEM((full, BLOCK), BF16),
            pltpu.VMEM((full + GROUPS * SHARE, BLOCK), BF16),
            pltpu.VMEM((full, BLOCK), BF16),
            pltpu.VMEM((full, BLOCK), BF16),
            pltpu.VMEM((width, rows), BF16),
            pltpu.VMEM((width, rows), BF16),
            pltpu.VMEM((NFILT, 1, rows), F32),
            pltpu.VMEM((CTX, 1, rows), F32),
            pltpu.VMEM((NBLOCK, BLOCK, BLOCK), BF16),
            pltpu.VMEM((full, BLOCK), F32),
            pltpu.VMEM((BLOCK, full), BF16),
            pltpu.VMEM((NBLOCK + 1, BLOCK, BLOCK), F32),
            pltpu.VMEM((CTX, 1, rows), F32),
            pltpu.VMEM((PLANES, RING, 1, rows), F32),
            pltpu.VMEM((RING, 1, rows), F32),
            pltpu.VMEM((nchan * RING, 1, rows), F32),
        ] + [dma((CTX,))] * 10 + [dma((PLANES,))] * 2 + [dma((nchan * RING,))] * 2,
        compiler_params=pltpu.CompilerParams(
            collective_id=0, has_side_effects=True, vmem_limit_bytes=40 * 1024 * 1024
        ),
    )(queries, keys, values, filters, cotangent)


def solution(mesh):
    act = P("ctx", "chan")
    taps = P(None, "ctx")
    return jax.shard_map(
        functools.partial(shards, mesh.shape["chan"]),
        mesh=mesh,
        in_specs=(act, act, act, taps, act),
        out_specs=(act, act, act, act, taps),
        check_vma=False,
    )
```

time: 849 us -> 59.5 us (0.07)
  waiting for transfers between devices: 481 us -> 0 us
  local copies, waits for them, and re-layouts: 259 us -> 7.86 us
  blocking collectives: 56 us -> 0 us
  Pallas kernels: 0 us -> 50.7 us
  loops' own time: 17.9 us -> 0 us
  matrix products: 15.2 us -> 0 us
  between operations: 14 us -> 0.66 us
    unnamed x4 -> x0, waiting for transfers between devices: 319 us -> none
    all_gather x2 -> x0, waiting for transfers between devices: 162 us -> none  [the longest x1 96.9 us: shards(): lax.all_gather(gated, 'ctx', axis=0, tiled=True)]
    reshape x22 -> x0, local copies, waits for them, and re-layouts: 77.3 us -> none  [the longest x9 56.2 us: toeplitz(): return flat.reshape(padded.shape[0], height, span - 1)[:, :, :breadth]]
    cond x37 -> x0, local copies, waits for them, and re-layouts: 76.6 us -> none
    pallas_call x0 -> x1, Pallas kernels: none -> 50.7 us  [shards(): pl.pallas_call(functools.partial(kernel, nchan, scale), out_shape=(act, a...]
    another operation x18 -> x0, local copies, waits for them, and re-layouts: 43.2 us -> none  [toeplitz(): tiled = jnp.tile(flipped, (1, height + 1))]
    all_gather x1 -> x0, blocking collectives: 38.3 us -> none  [shards(): taps = lax.all_gather(filters, 'ctx', axis=1, tiled=True)]
    slice x11 -> x0, local copies, waits for them, and re-layouts: 25.6 us -> none  [the longest x9 24.4 us: toeplitz(): flat = tiled[:, height - 1:height - 1 + height * (span - 1)]]
  transfers between devices with their start and end apart: 3 -> 0, of which waited for: 3 -> 0; matrix products, arithmetic and copies ran while one was open for 1% -> 0% of each run, Pallas kernels for 0% -> 0%
where the time goes in v1:
time: 59.5 us; the launch traced here: 59.2 us
  Pallas kernels  50.7 us (85%)
  local copies, waits for them, and re-layouts  7.86 us (13%)
  between operations  0.66 us (1%)
    pallas_call x1, Pallas kernels, shards(): pl.pallas_call(functools.partial(kernel, nchan, scale), out_shape=(act, a...  50.7 us
    unnamed x15, local copies, waits for them, and re-layouts  7.86 us

profile of v1, /device:TPU:1, one launch (start us, length us, event | category | flops | bytes accessed | tf_op | source)
XLA Modules:
  0.0 59.2 jit_solution(3599797543537228110)
XLA Ops:
  0.6 0.0 copy-start
  0.6 0.9 %copy-done = bf16[128,1024]{1,0:T(8,128)(2,1)S(1)} copy-done((bf16[128,1024]{1,0:T(8,128)(2,1)S(1)}, bf16[128,1024]{1,0:T(8,128)(2,1)}, u32[]{:S(2)}) %copy-start) | copy-done | bytes 262168
  1.6 0.0 copy-start.1
  1.6 0.9 %copy-done.1 = bf16[128,1024]{1,0:T(8,128)(2,1)S(1)} copy-done((bf16[128,1024]{1,0:T(8,128)(2,1)S(1)}, bf16[128,1024]{1,0:T(8,128)(2,1)}, u32[]{:S(2)}) %copy-start.1) | copy-done | bytes 262168
  2.5 0.0 copy-start.2
  2.5 0.9 %copy-done.2 = bf16[128,1024]{1,0:T(8,128)(2,1)S(1)} copy-done((bf16[128,1024]{1,0:T(8,128)(2,1)S(1)}, bf16[128,1024]{1,0:T(8,128)(2,1)}, u32[]{:S(2)}) %copy-start.2) | copy-done | bytes 262168
  3.5 0.0 copy-start.3
  3.5 0.9 %copy-done.3 = bf16[128,1024]{1,0:T(8,128)(2,1)S(1)} copy-done((bf16[128,1024]{1,0:T(8,128)(2,1)S(1)}, bf16[128,1024]{1,0:T(8,128)(2,1)}, u32[]{:S(2)}) %copy-start.3) | copy-done | bytes 262168
  4.4 0.0 copy-start.4
  4.4 0.7 %copy-done.4 = bf16[4,128]{1,0:T(4,128)(2,1)S(1)} copy-done((bf16[4,128]{1,0:T(4,128)(2,1)S(1)}, bf16[4,128]{1,0:T(4,128)(2,1)}, u32[]{:S(2)}) %copy-start.4) | copy-done | bytes 1048
  5.1 50.7 %shard_map.92 = (bf16[128,1024]{1,0:T(8,128)(2,1)S(1)}, bf16[128,1024]{1,0:T(8,128)(2,1)S(1)}, bf16[128,1024]{1,0:T(8,128)(2,1)S(1)}, bf16[128,1024]{1,0:T(8,128)(2,1)S(1)}, f32[4,128]{1,0:T(4,128)S(1)}) custom-call(bf16[128,1024]{1,0:T(8,128)(2,1)S(1)} %copy-done, bf16[128,1024]{1,0:T(8,128)(2,1)S(1)} %copy-done.1, bf16[128,1024]{1,0:T(8,128)(2,1)S(1)} %copy-done.2, ...), custom_call_target="tpu_custom_call" | custom-call | tf_op jit(solution)/shard_map/pallas_call | solution.py:265
  55.9 0.7 %copy.15 = bf16[128,1024]{1,0:T(8,128)(2,1)} copy(bf16[128,1024]{1,0:T(8,128)(2,1)S(1)} %get-tuple-element.10) | data formatting | bytes 524288
  56.6 0.7 %copy.16 = bf16[128,1024]{1,0:T(8,128)(2,1)} copy(bf16[128,1024]{1,0:T(8,128)(2,1)S(1)} %get-tuple-element.11) | data formatting | bytes 524288
  57.3 0.7 %copy.17 = bf16[128,1024]{1,0:T(8,128)(2,1)} copy(bf16[128,1024]{1,0:T(8,128)(2,1)S(1)} %get-tuple-element.12) | data formatting | bytes 524288
  58.0 0.7 %copy.18 = bf16[128,1024]{1,0:T(8,128)(2,1)} copy(bf16[128,1024]{1,0:T(8,128)(2,1)S(1)} %get-tuple-element.13) | data formatting | bytes 524288
  58.7 0.6 copy.19
Async XLA Ops:
  0.6 1.0 %copy-start = (bf16[128,1024]{1,0:T(8,128)(2,1)S(1)}, bf16[128,1024]{1,0:T(8,128)(2,1)}, u32[]{:S(2)}) copy-start(bf16[128,1024]{1,0:T(8,128)(2,1)} %q_ref.1) | copy-start | bytes 786436
  1.6 0.9 %copy-start.1 = (bf16[128,1024]{1,0:T(8,128)(2,1)S(1)}, bf16[128,1024]{1,0:T(8,128)(2,1)}, u32[]{:S(2)}) copy-start(bf16[128,1024]{1,0:T(8,128)(2,1)} %k_ref.1) | copy-start | bytes 786436
  2.5 0.9 %copy-start.2 = (bf16[128,1024]{1,0:T(8,128)(2,1)S(1)}, bf16[128,1024]{1,0:T(8,128)(2,1)}, u32[]{:S(2)}) copy-start(bf16[128,1024]{1,0:T(8,128)(2,1)} %v_ref.1) | copy-start | bytes 786436
  3.5 0.9 %copy-start.3 = (bf16[128,1024]{1,0:T(8,128)(2,1)S(1)}, bf16[128,1024]{1,0:T(8,128)(2,1)}, u32[]{:S(2)}) copy-start(bf16[128,1024]{1,0:T(8,128)(2,1)} %c_ref.1) | copy-start | bytes 786436
  4.4 0.7 %copy-start.4 = (bf16[4,128]{1,0:T(4,128)(2,1)S(1)}, bf16[4,128]{1,0:T(4,128)(2,1)}, u32[]{:S(2)}) copy-start(bf16[4,128]{1,0:T(4,128)(2,1)} %taps_ref.1) | copy-start | bytes 3076

commit v2 on v1

--- a/solution.py
+++ b/solution.py
@@ -26,8 +26,9 @@
 
 
 def kernel(nchan, scale,
-           q_ref, k_ref, v_ref, taps_ref, c_ref,
+           q_hbm, k_hbm, v_hbm, taps_hbm, c_hbm,
            out_ref, qg_ref, kg_ref, vg_ref, fg_ref,
+           q_ref, k_ref, v_ref, taps_ref, c_ref, load_sem,
            sg, sb, rg, rb, om, og, bm, bg, ts, tr, toep, acc, gt_t, prod, fa, ra, sbuf, rf,
            t_ss, t_rs, g_ss, g_rs, b_ss, b_rs, m_ss, m_rs, o_ss, o_rs, a_ss, a_rs, f_ss, f_rs):
     ch = lax.axis_index("chan")
@@ -71,10 +72,17 @@
 
     lax.fori_loop(RING, nchan * RING, greet_plane, 0)
 
+    loads = [pltpu.make_async_copy(src, dst, load_sem.at[n]) for n, (src, dst) in enumerate((
+        (k_hbm, k_ref), (v_hbm, v_ref), (c_hbm, c_ref), (q_hbm, q_ref), (taps_hbm, taps_ref)))]
+    for load in loads:
+        load.start()
+
     row = lax.broadcasted_iota(jnp.int32, (128, 128), 0)
     lane = lax.broadcasted_iota(jnp.int32, (128, 128), 1)
     order = (lane == NFILT * (row % SHARE) + row // SHARE).astype(BF16)
 
+    for load in loads:
+        load.wait()
     for f in range(NFILT):
         ts[f] = taps_ref[f:f + 1, :].astype(F32)
     for g in range(PLANES):
@@ -166,6 +174,38 @@
     bm[chunk(me), :] = om[my_rows, my_lanes]
 
     recv_all(b_copy)
+    flip = (sub + col == BLOCK - 1).astype(BF16)
+    gt_t[...] = dot(flip, rg[...], 1, 1).astype(BF16)
+    for group in range(NBLOCK // GROUPS):
+        depth = full - group * GROUPS * SHARE
+        for s in range(GROUPS):
+            d = group * GROUPS + s
+            prod[d] = dot(gt_t[:, 0:depth], rb[SHARE * d:SHARE * d + depth, :], 1, 0)
+    prod[NBLOCK] = jnp.zeros((BLOCK, BLOCK), F32)
+
+    def lag_sums(plane, carry):
+        for e in range(2):
+            d = 2 * plane + e
+            both = jnp.where(col + sub >= BLOCK - 1, prod[d], prod[d + 1])
+            sums = jnp.sum(pltpu.roll(both, 1, 1, stride=1, stride_axis=0), axis=0, keepdims=True)
+            fa[RING * plane + 2 * e] = sums[:, 0:128]
+            fa[RING * plane + 2 * e + 1] = sums[:, 128:256]
+        return carry
+
+    lax.fori_loop(0, PLANES, lag_sums, 0)
+
+    def a_copy(p, src, slot):
+        return copy(fa.at[pl.ds(RING * p, RING)], ra.at[src], a_ss.at[p], a_rs.at[slot], RING * p + y)
+
+    def planes(fn):
+        def body(step, carry):
+            fn(lax.rem(z + step, PLANES))
+            return carry
+        lax.fori_loop(1, PLANES, body, 0)
+
+    planes(lambda p: a_copy(p, z, z).start())
+    ra[z] = fa[pl.ds(RING * z, RING)]
+
     for d in range(NBLOCK):
         part = dot(rb[SHARE * d:full, :], toep[d], 1, 1)
         if d == 0:
@@ -176,44 +216,33 @@
     send_all(o_copy)
     bg[chunk(me), :] = og[my_rows, my_lanes]
 
-    flip = (sub + col == BLOCK - 1).astype(BF16)
-    gt_t[...] = dot(flip, rg[...], 1, 1).astype(BF16)
-    for group in range(NBLOCK // GROUPS):
-        depth = full - group * GROUPS * SHARE
-        for s in range(GROUPS):
-            d = group * GROUPS + s
-            prod[d] = dot(gt_t[:, 0:depth], rb[SHARE * d:SHARE * d + depth, :], 1, 0)
-    prod[NBLOCK] = jnp.zeros((BLOCK, BLOCK), F32)
-
-    def lag_sums(plane, carry):
-        for e in range(2):
-            d = 2 * plane + e
-            both = jnp.where(col + sub >= BLOCK - 1, prod[d], prod[d + 1])
-            sums = jnp.sum(pltpu.roll(both, 1, 1, stride=1, stride_axis=0), axis=0, keepdims=True)
-            fa[RING * plane + 2 * e] = sums[:, 0:128]
-            fa[RING * plane + 2 * e + 1] = sums[:, 128:256]
-        return carry
-
-    lax.fori_loop(0, PLANES, lag_sums, 0)
-
-    def a_copy(p, src, slot):
-        return copy(fa.at[pl.ds(RING * p, RING)], ra.at[src], a_ss.at[p], a_rs.at[slot], RING * p + y)
-
-    def planes(fn):
-        def body(step, carry):
-            fn(lax.rem(z + step, PLANES))
-            return carry
-        lax.fori_loop(1, PLANES, body, 0)
-
-    planes(lambda p: a_copy(p, z, z).start())
-    ra[z] = fa[pl.ds(RING * z, RING)]
-
-    recv_all(m_copy)
-    for g in range(PLANES):
-        at = slice(g * 128, (g + 1) * 128)
+    def tiles(make, fn):
+        def pieces(step, carry):
+            i = peer(step)
+            make(i, i, i).wait_recv()
+            return carry
+
+        def body(n, carry):
+            lax.fori_loop(RING * n, RING * n + RING, pieces, 0)
+            g = lax.div(peer(RING * n), RING)
+            fn(pl.ds(pl.multiple_of(g * 128, 128), 128))
+            return carry
+
+        lax.fori_loop(0, PLANES - 1, body, 0)
+        lax.fori_loop(CTX - RING + 1, CTX, pieces, 0)
+        fn(pl.ds(pl.multiple_of(z * 128, 128), 128))
+
+    def finish_mixed(at):
         mixed = dot(bm[at, :], order, 0, 0)
         out_ref[:, at] = (q_ref[:, at].astype(F32) * mixed).astype(BF16)
         qg_ref[:, at] = (c_ref[:, at].astype(F32) * mixed).astype(BF16)
+
+    def finish_grad(at):
+        grad = dot(bg[at, :], order, 0, 0)
+        kg_ref[:, at] = (grad * v_ref[:, at].astype(F32)).astype(BF16)
+        vg_ref[:, at] = (grad * k_ref[:, at].astype(F32)).astype(BF16)
+
+    tiles(m_copy, finish_mixed)
 
     planes(lambda p: a_copy(p, p, p).wait_recv())
     total = ra[0]
@@ -231,12 +260,7 @@
     each_plane_peer(lambda p, r: f_copy(p, r, ch, y).start())
     rf[pl.ds(ch * RING + y, 1)] = sbuf[pl.ds(y, 1)]
 
-    recv_all(o_copy)
-    for g in range(PLANES):
-        at = slice(g * 128, (g + 1) * 128)
-        grad = dot(bg[at, :], order, 0, 0)
-        kg_ref[:, at] = (grad * v_ref[:, at].astype(F32)).astype(BF16)
-        vg_ref[:, at] = (grad * k_ref[:, at].astype(F32)).astype(BF16)
+    tiles(o_copy, finish_grad)
 
     each_plane_peer(lambda p, r: f_copy(p, r, p, r).wait_recv())
     for f in range(NFILT):
@@ -252,6 +276,15 @@
     sent_all(o_copy)
     planes(lambda p: a_copy(p, z, z).wait_send())
     each_plane_peer(lambda p, r: f_copy(p, r, ch, y).wait_send())
+
+
+def store(*refs):
+    sems = refs[10]
+    copies = [pltpu.make_async_copy(refs[n], refs[5 + n], sems.at[n]) for n in range(5)]
+    for item in copies:
+        item.start()
+    for item in copies:
+        item.wait()
 
 
 def shards(nchan, queries, keys, values, filters, cotangent):
@@ -262,12 +295,19 @@
     dma = pltpu.SemaphoreType.DMA
     full = NBLOCK * SHARE
     act = jax.ShapeDtypeStruct((rows, width), BF16)
-    return pl.pallas_call(
+    queries, keys, values, filters, cotangent = [pltpu.with_memory_space_constraint(x, pltpu.HBM) for x in (queries, keys, values, filters, cotangent)]
+    held = pl.pallas_call(
         functools.partial(kernel, nchan, scale),
         out_shape=(act, act, act, act, jax.ShapeDtypeStruct((NFILT, rows), F32)),
-        in_specs=[vmem] * 5,
+        in_specs=[pl.BlockSpec(memory_space=pltpu.HBM)] * 5,
         out_specs=[vmem] * 5,
         scratch_shapes=[
+            pltpu.VMEM((rows, width), BF16),
+            pltpu.VMEM((rows, width), BF16),
+            pltpu.VMEM((rows, width), BF16),
+            pltpu.VMEM((NFILT, rows), BF16),
+            pltpu.VMEM((rows, width), BF16),
+            dma((5,)),
             pltpu.VMEM((width, rows), BF16),
             pltpu.VMEM((width, rows), BF16),
             pltpu.VMEM((full, BLOCK), BF16),
@@ -288,9 +328,17 @@
             pltpu.VMEM((nchan * RING, 1, rows), F32),
         ] + [dma((CTX,))] * 10 + [dma((PLANES,))] * 2 + [dma((nchan * RING,))] * 2,
         compiler_params=pltpu.CompilerParams(
-            collective_id=0, has_side_effects=True, vmem_limit_bytes=40 * 1024 * 1024
+            collective_id=0, has_side_effects=True, vmem_limit_bytes=40000000
         ),
     )(queries, keys, values, filters, cotangent)
+    return pl.pallas_call(
+        store,
+        out_shape=(act, act, act, act, jax.ShapeDtypeStruct((NFILT, rows), F32)),
+        in_specs=[vmem] * 5,
+        out_specs=[pl.BlockSpec(memory_space=pltpu.HBM)] * 5,
+        scratch_shapes=[dma((5,))],
+        compiler_params=pltpu.CompilerParams(vmem_limit_bytes=4 * 1024 * 1024),
+    )(*held)
 
 
 def solution(mesh):

time: 59.5 us -> 51.6 us (0.87)
  local copies, waits for them, and re-layouts: 7.86 us -> 0 us
    unnamed x15 -> x0, local copies, waits for them, and re-layouts: 7.86 us -> none
    pallas_call x0 -> x1, Pallas kernels: none -> 1.01 us  [shards(): pl.pallas_call(store, out_shape=(act, act, act, act, jax.ShapeDtypeStruct...]
    pallas_call x1, Pallas kernels: 50.7 us -> 49.8 us  [shards(): pl.pallas_call(functools.partial(kernel, nchan, scale), out_shape=(act, a...]
where the time goes in v2:
time: 51.6 us; the launch traced here: 51.5 us
  Pallas kernels  50.8 us (98%)
  between operations  0.64 us (1%)
    pallas_call x1, Pallas kernels, shards(): pl.pallas_call(functools.partial(kernel, nchan, scale), out_shape=(act, a...  49.8 us

profile of v2, /device:TPU:1, one launch (start us, length us, event | category | flops | bytes accessed | tf_op | source)
XLA Modules:
  0.0 51.5 jit_solution(1962164153187899887)
XLA Ops:
  0.6 49.8 %shard_map.92 = (bf16[128,1024]{1,0:T(8,128)(2,1)S(1)}, bf16[128,1024]{1,0:T(8,128)(2,1)S(1)}, bf16[128,1024]{1,0:T(8,128)(2,1)S(1)}, bf16[128,1024]{1,0:T(8,128)(2,1)S(1)}, f32[4,128]{1,0:T(4,128)S(1)}) custom-call(bf16[128,1024]{1,0:T(8,128)(2,1)} %q_hbm.1, bf16[128,1024]{1,0:T(8,128)(2,1)} %k_hbm.1, bf16[128,1024]{1,0:T(8,128)(2,1)} %v_hbm.1, ...), custom_call_target="tpu_custom_call" | custom-call | tf_op jit(solution)/shard_map/pallas_call | solution.py:299
  50.4 1.0 %shard_map.93 = (bf16[128,1024]{1,0:T(8,128)(2,1)}, bf16[128,1024]{1,0:T(8,128)(2,1)}, bf16[128,1024]{1,0:T(8,128)(2,1)}, bf16[128,1024]{1,0:T(8,128)(2,1)}, f32[4,128]{1,0:T(4,128)}) custom-call(bf16[128,1024]{1,0:T(8,128)(2,1)S(1)} %get-tuple-element.10.refs_0_, bf16[128,1024]{1,0:T(8,128)(2,1)S(1)} %get-tuple-element.11.refs_1_, ...), custom_call_target="tpu_custom_call" | custom-call | tf_op jit(solution)/shard_map/pallas_call | solution.py:334

commit v3 on v2

--- a/solution.py
+++ b/solution.py
@@ -30,47 +30,28 @@
            out_ref, qg_ref, kg_ref, vg_ref, fg_ref,
            q_ref, k_ref, v_ref, taps_ref, c_ref, load_sem,
            sg, sb, rg, rb, om, og, bm, bg, ts, tr, toep, acc, gt_t, prod, fa, ra, sbuf, rf,
-           t_ss, t_rs, g_ss, g_rs, b_ss, b_rs, m_ss, m_rs, o_ss, o_rs, a_ss, a_rs, f_ss, f_rs):
+           send_sem, t_rs, g_rs, b_rs, m_rs, o_rs, a_rs, f_rs):
     ch = lax.axis_index("chan")
     me = lax.axis_index("ctx")
     z = lax.div(me, RING)
     y = lax.rem(me, RING)
-
-    def peer(step):
-        n = lax.div(step, RING)
-        half = lax.div(n + 1, 2)
-        dz = lax.rem(PLANES // 2 + PLANES + (1 - 2 * lax.rem(n, 2)) * half, PLANES)
-        dy = lax.rem(step, RING)
-        return lax.rem(z + dz, PLANES) * RING + lax.rem(y + dy, RING)
-
-    def each_peer(fn):
-        def body(step, carry):
-            fn(peer(step))
-            return carry
-        lax.fori_loop(0, CTX - RING, body, 0)
-        lax.fori_loop(CTX - RING + 1, CTX, body, 0)
-
-    def each_plane_peer(fn):
-        def body(step, carry):
-            p = lax.rem(ch + lax.div(step, RING), nchan)
-            fn(p, lax.rem(y + lax.rem(step, RING), RING))
-            return carry
-        lax.fori_loop(1, nchan * RING, body, 0)
+    zs = [z] + [lax.rem(z + dz, PLANES) for dz in range(1, PLANES)]
+    ys = [y] + [lax.rem(y + dy, RING) for dy in range(1, RING)]
+    ps = [ch] + [lax.rem(ch + p, nchan) for p in range(1, nchan)]
+    planes = (4, 3, 5, 2, 6, 1, 7, 0)
+    peers = [(dz, dy) for dz in planes for dy in range(RING) if dz or dy]
+    near = [(p, dy) for p in range(nchan) for dy in range(RING) if p or dy]
 
     barrier = pltpu.get_barrier_semaphore()
 
-    def greet(i):
-        pl.semaphore_signal(barrier, inc=1, device_id=(ch, i), device_id_type=MESH)
-
-    each_peer(greet)
-
-    def greet_plane(step, carry):
-        p = lax.rem(ch + lax.div(step, RING), nchan)
-        pl.semaphore_signal(barrier, inc=1, device_id=(p, z * RING + lax.rem(step, RING)),
-                            device_id_type=MESH)
-        return carry
-
-    lax.fori_loop(RING, nchan * RING, greet_plane, 0)
+    def greet(p, dz, dy):
+        pl.semaphore_signal(barrier, inc=1, device_id=(ps[p], zs[dz] * RING + ys[dy]), device_id_type=MESH)
+
+    for dz, dy in peers:
+        greet(0, dz, dy)
+    for p in range(1, nchan):
+        for dy in range(RING):
+            greet(p, 0, dy)
 
     loads = [pltpu.make_async_copy(src, dst, load_sem.at[n]) for n, (src, dst) in enumerate((
         (k_hbm, k_ref), (v_hbm, v_ref), (c_hbm, c_ref), (q_hbm, q_ref), (taps_hbm, taps_ref)))]
@@ -101,51 +82,42 @@
         return (pl.ds(pl.multiple_of(lax.div(i, 2) * SHARE, SHARE), SHARE),
                 pl.ds(pl.multiple_of(lax.rem(i, 2) * 128, 128), 128))
 
-    def copy(src, dst, ss, rs, i):
-        return pltpu.make_async_remote_copy(src_ref=src, dst_ref=dst, send_sem=ss, recv_sem=rs,
-                                            device_id=(ch, i), device_id_type=MESH)
-
-    def taps_copy(i, src, slot):
-        return copy(ts.at[pl.ds(lax.rem(i, RING), 1)], tr.at[pl.ds(src, 1)], t_ss.at[i], t_rs.at[slot], i)
-
-    def in_copy(send, recv, ss, rs):
-        def make(i, src, slot):
-            r, l = place(src)
-            return copy(send.at[chunk(i), :], recv.at[r, l], ss.at[i], rs.at[slot], i)
-        return make
-
-    def out_copy(send, recv, ss, rs):
-        def make(i, src, slot):
-            r, l = place(i)
-            return copy(send.at[r, l], recv.at[chunk(src), :], ss.at[i], rs.at[slot], i)
-        return make
-
-    g_copy = in_copy(sg, rg, g_ss, g_rs)
-    b_copy = in_copy(sb, rb, b_ss, b_rs)
-    m_copy = out_copy(om, bm, m_ss, m_rs)
-    o_copy = out_copy(og, bg, o_ss, o_rs)
-
-    def send_all(make):
-        each_peer(lambda i: make(i, me, me).start())
-
-    def recv_all(make):
-        each_peer(lambda i: make(i, i, i).wait_recv())
-
-    def sent_all(make):
-        each_peer(lambda i: make(i, me, me).wait_send())
-
-    send_all(taps_copy)
-    send_all(g_copy)
-    send_all(b_copy)
+    my_rows, my_lanes = place(me)
+    places = {(dz, dy): place(zs[dz] * RING + ys[dy]) for dz, dy in peers}
+
+    def copy(src, dst, n, recv, p, dz, dy):
+        return pltpu.make_async_remote_copy(
+            src_ref=src, dst_ref=dst, send_sem=send_sem.at[n], recv_sem=recv,
+            device_id=(ps[p], zs[dz] * RING + ys[dy]), device_id_type=MESH)
+
+    def arrived(like, recv):
+        copy(like, like, 0, recv, 0, 1, 0).wait_recv()
+
+    def sent(like, n):
+        copy(like, like, n, t_rs.at[0], 0, 1, 0).wait_send()
+
+    def send_in(send, recv, n, rs):
+        for dz, dy in peers:
+            copy(send.at[chunk(zs[dz] * RING + ys[dy]), :], recv.at[my_rows, my_lanes], n, rs.at[0], 0, dz, dy).start()
+
+    def send_out(send, recv, n, rs):
+        for dz, dy in peers:
+            r, l = places[dz, dy]
+            copy(send.at[r, l], recv.at[chunk(me), :], n, rs.at[(PLANES - dz) % PLANES], 0, dz, dy).start()
+
+    others = pl.ds(0, (CTX - 1) * SHARE)
+    for dz, dy in peers:
+        copy(ts.at[pl.ds(ys[dy], 1)], tr.at[pl.ds(me, 1)], 0, t_rs.at[0], 0, dz, dy).start()
+    send_in(sg, rg, 1, g_rs)
+    send_in(sb, rb, 2, b_rs)
 
     pad = GROUPS * SHARE
-    my_rows, my_lanes = place(me)
     tr[pl.ds(me, 1)] = ts[pl.ds(y, 1)]
     rg[my_rows, my_lanes] = sg[chunk(me), :]
     rb[my_rows, my_lanes] = sb[chunk(me), :]
     rb[NBLOCK * SHARE:NBLOCK * SHARE + pad, :] = jnp.zeros((pad, BLOCK), BF16)
 
-    recv_all(taps_copy)
+    arrived(tr.at[pl.ds(0, CTX - 1)], t_rs.at[0])
     sub = lax.broadcasted_iota(jnp.int32, (BLOCK, BLOCK), 0)
     col = lax.broadcasted_iota(jnp.int32, (BLOCK, BLOCK), 1)
 
@@ -162,7 +134,7 @@
     lax.fori_loop(0, NBLOCK, build, 0)
 
     full = NBLOCK * SHARE
-    recv_all(g_copy)
+    arrived(sg.at[others], g_rs.at[0])
     for d in range(NBLOCK):
         part = dot(rg[0:full - SHARE * d, :], toep[d], 1, 0)
         if d == 0:
@@ -170,12 +142,12 @@
         else:
             acc[SHARE * d:full, :] += part
     om[...] = acc[...].astype(BF16)
-    send_all(m_copy)
+    send_out(om, bm, 3, m_rs)
     bm[chunk(me), :] = om[my_rows, my_lanes]
 
-    recv_all(b_copy)
     flip = (sub + col == BLOCK - 1).astype(BF16)
     gt_t[...] = dot(flip, rg[...], 1, 1).astype(BF16)
+    arrived(sb.at[others], b_rs.at[0])
     for group in range(NBLOCK // GROUPS):
         depth = full - group * GROUPS * SHARE
         for s in range(GROUPS):
@@ -194,16 +166,8 @@
 
     lax.fori_loop(0, PLANES, lag_sums, 0)
 
-    def a_copy(p, src, slot):
-        return copy(fa.at[pl.ds(RING * p, RING)], ra.at[src], a_ss.at[p], a_rs.at[slot], RING * p + y)
-
-    def planes(fn):
-        def body(step, carry):
-            fn(lax.rem(z + step, PLANES))
-            return carry
-        lax.fori_loop(1, PLANES, body, 0)
-
-    planes(lambda p: a_copy(p, z, z).start())
+    for dz in planes[:-1]:
+        copy(fa.at[pl.ds(RING * zs[dz], RING)], ra.at[z], 5, a_rs.at[0], 0, dz, 0).start()
     ra[z] = fa[pl.ds(RING * z, RING)]
 
     for d in range(NBLOCK):
@@ -213,69 +177,47 @@
         else:
             acc[0:full - SHARE * d, :] += part
     og[...] = acc[...].astype(BF16)
-    send_all(o_copy)
+    send_out(og, bg, 4, o_rs)
     bg[chunk(me), :] = og[my_rows, my_lanes]
 
-    def tiles(make, fn):
-        def pieces(step, carry):
-            i = peer(step)
-            make(i, i, i).wait_recv()
-            return carry
-
-        def body(n, carry):
-            lax.fori_loop(RING * n, RING * n + RING, pieces, 0)
-            g = lax.div(peer(RING * n), RING)
-            fn(pl.ds(pl.multiple_of(g * 128, 128), 128))
-            return carry
-
-        lax.fori_loop(0, PLANES - 1, body, 0)
-        lax.fori_loop(CTX - RING + 1, CTX, pieces, 0)
-        fn(pl.ds(pl.multiple_of(z * 128, 128), 128))
-
-    def finish_mixed(at):
-        mixed = dot(bm[at, :], order, 0, 0)
+    def tiles(recv, rs, fn):
+        for dz in planes:
+            arrived(recv.at[pl.ds(0, (RING - (dz == 0)) * SHARE), :], rs.at[dz])
+            rows = pl.ds(pl.multiple_of(zs[dz] * 128, 128), 128)
+            fn(dot(recv[rows, :], order, 0, 0), rows)
+
+    def finish_mixed(mixed, at):
         out_ref[:, at] = (q_ref[:, at].astype(F32) * mixed).astype(BF16)
         qg_ref[:, at] = (c_ref[:, at].astype(F32) * mixed).astype(BF16)
 
-    def finish_grad(at):
-        grad = dot(bg[at, :], order, 0, 0)
+    def finish_grad(grad, at):
         kg_ref[:, at] = (grad * v_ref[:, at].astype(F32)).astype(BF16)
         vg_ref[:, at] = (grad * k_ref[:, at].astype(F32)).astype(BF16)
 
-    tiles(m_copy, finish_mixed)
-
-    planes(lambda p: a_copy(p, p, p).wait_recv())
+    arrived(fa.at[pl.ds(0, (PLANES - 1) * RING)], a_rs.at[0])
     total = ra[0]
     for p in range(1, PLANES):
         total = total + ra[p]
     sbuf[...] = total
-
-    def f_copy(p, r, srcp, srcf):
-        slot = srcp * RING + srcf
-        return pltpu.make_async_remote_copy(
-            src_ref=sbuf.at[pl.ds(r, 1)], dst_ref=rf.at[pl.ds(slot, 1)],
-            send_sem=f_ss.at[p * RING + r], recv_sem=f_rs.at[slot],
-            device_id=(p, z * RING + r), device_id_type=MESH)
-
-    each_plane_peer(lambda p, r: f_copy(p, r, ch, y).start())
+    for p, dy in near:
+        copy(sbuf.at[pl.ds(ys[dy], 1)], rf.at[pl.ds(ch * RING + y, 1)], 6, f_rs.at[0], p, 0, dy).start()
     rf[pl.ds(ch * RING + y, 1)] = sbuf[pl.ds(y, 1)]
 
-    tiles(o_copy, finish_grad)
-
-    each_plane_peer(lambda p, r: f_copy(p, r, p, r).wait_recv())
+    tiles(bm, m_rs, finish_mixed)
+    tiles(bg, o_rs, finish_grad)
+
+    arrived(rf.at[pl.ds(0, nchan * RING - 1)], f_rs.at[0])
     for f in range(NFILT):
         total = rf[f]
         for p in range(1, nchan):
             total = total + rf[p * RING + f]
         fg_ref[f:f + 1, :] = total * scale
 
-    sent_all(taps_copy)
-    sent_all(g_copy)
-    sent_all(b_copy)
-    sent_all(m_copy)
-    sent_all(o_copy)
-    planes(lambda p: a_copy(p, z, z).wait_send())
-    each_plane_peer(lambda p, r: f_copy(p, r, ch, y).wait_send())
+    sent(tr.at[pl.ds(0, CTX - 1)], 0)
+    for n in range(1, 5):
+        sent(sg.at[others], n)
+    sent(fa.at[pl.ds(0, (PLANES - 1) * RING)], 5)
+    sent(rf.at[pl.ds(0, nchan * RING - 1)], 6)
 
 
 def store(*refs):
@@ -326,7 +268,7 @@
             pltpu.VMEM((PLANES, RING, 1, rows), F32),
             pltpu.VMEM((RING, 1, rows), F32),
             pltpu.VMEM((nchan * RING, 1, rows), F32),
-        ] + [dma((CTX,))] * 10 + [dma((PLANES,))] * 2 + [dma((nchan * RING,))] * 2,
+        ] + [dma((7,))] + [dma((1,))] * 3 + [dma((PLANES,))] * 2 + [dma((1,))] * 2,
         compiler_params=pltpu.CompilerParams(
             collective_id=0, has_side_effects=True, vmem_limit_bytes=40000000
         ),

time: 51.6 us -> 43.3 us (0.84)
  Pallas kernels: 50.8 us -> 42.6 us
    pallas_call x1, Pallas kernels: 49.8 us -> 41.5 us  [shards(): pl.pallas_call(functools.partial(kernel, nchan, scale), out_shape=(act, a...]
where the time goes in v3:
time: 43.3 us; the launch traced here: 43.2 us
  Pallas kernels  42.6 us (98%)
  between operations  0.64 us (1%)
    pallas_call x1, Pallas kernels, shards(): pl.pallas_call(functools.partial(kernel, nchan, scale), out_shape=(act, a...  41.5 us
    pallas_call x1, Pallas kernels, shards(): pl.pallas_call(store, out_shape=(act, act, act, act, jax.ShapeDtypeStruct...  1.01 us

profile of v3, /device:TPU:1, one launch (start us, length us, event | category | flops | bytes accessed | tf_op | source)
XLA Modules:
  0.0 43.2 jit_solution(15611790797267048457)
XLA Ops:
  0.6 41.5 %shard_map.92 = (bf16[128,1024]{1,0:T(8,128)(2,1)S(1)}, bf16[128,1024]{1,0:T(8,128)(2,1)S(1)}, bf16[128,1024]{1,0:T(8,128)(2,1)S(1)}, bf16[128,1024]{1,0:T(8,128)(2,1)S(1)}, f32[4,128]{1,0:T(4,128)S(1)}) custom-call(bf16[128,1024]{1,0:T(8,128)(2,1)} %q_hbm.1, bf16[128,1024]{1,0:T(8,128)(2,1)} %k_hbm.1, bf16[128,1024]{1,0:T(8,128)(2,1)} %v_hbm.1, ...), custom_call_target="tpu_custom_call" | custom-call | tf_op jit(solution)/shard_map/pallas_call | solution.py:241
  42.2 1.0 %shard_map.93 = (bf16[128,1024]{1,0:T(8,128)(2,1)}, bf16[128,1024]{1,0:T(8,128)(2,1)}, bf16[128,1024]{1,0:T(8,128)(2,1)}, bf16[128,1024]{1,0:T(8,128)(2,1)}, f32[4,128]{1,0:T(4,128)}) custom-call(bf16[128,1024]{1,0:T(8,128)(2,1)S(1)} %get-tuple-element.10.refs_0_, bf16[128,1024]{1,0:T(8,128)(2,1)S(1)} %get-tuple-element.11.refs_1_, ...), custom_call_target="tpu_custom_call" | custom-call | tf_op jit(solution)/shard_map/pallas_call | solution.py:276

commit v4 on v3

--- a/solution.py
+++ b/solution.py
@@ -106,9 +106,9 @@
             copy(send.at[r, l], recv.at[chunk(me), :], n, rs.at[(PLANES - dz) % PLANES], 0, dz, dy).start()
 
     others = pl.ds(0, (CTX - 1) * SHARE)
+    send_in(sg, rg, 1, g_rs)
     for dz, dy in peers:
         copy(ts.at[pl.ds(ys[dy], 1)], tr.at[pl.ds(me, 1)], 0, t_rs.at[0], 0, dz, dy).start()
-    send_in(sg, rg, 1, g_rs)
     send_in(sb, rb, 2, b_rs)
 
     pad = GROUPS * SHARE
@@ -118,17 +118,20 @@
     rb[NBLOCK * SHARE:NBLOCK * SHARE + pad, :] = jnp.zeros((pad, BLOCK), BF16)
 
     arrived(tr.at[pl.ds(0, CTX - 1)], t_rs.at[0])
-    sub = lax.broadcasted_iota(jnp.int32, (BLOCK, BLOCK), 0)
-    col = lax.broadcasted_iota(jnp.int32, (BLOCK, BLOCK), 1)
+    toep[0, 128:256, 0:128] = jnp.zeros((128, 128), BF16)
+
+    def lag_block(e, this, last):
+        picked = jnp.where(row + lane < 128, jnp.broadcast_to(this, (128, 128)), jnp.broadcast_to(last, (128, 128)))
+        return pltpu.roll(picked, 0, 1, stride=1, stride_axis=0).astype(BF16)
 
     def build(d, carry):
-        this = jnp.concatenate([tr[2 * d], tr[2 * d + 1]], axis=1)
-        low = lax.max(d - 1, 0)
-        last = jnp.concatenate([tr[2 * low], tr[2 * low + 1]], axis=1)
-        last = last * (d > 0).astype(F32)
-        picked = jnp.where(sub + col < BLOCK, jnp.broadcast_to(this, (BLOCK, BLOCK)),
-                           jnp.broadcast_to(last, (BLOCK, BLOCK)))
-        toep[d] = pltpu.roll(picked, 0, 1, stride=1, stride_axis=0).astype(BF16)
+        low = lax.max(2 * d - 1, 0)
+        even = lag_block(2 * d, tr[2 * d], tr[low] * (d > 0).astype(F32))
+        odd = lag_block(2 * d + 1, tr[2 * d + 1], tr[2 * d])
+        toep[d, 0:128, 0:128] = even
+        toep[d, 128:256, 128:256] = even
+        toep[d, 0:128, 128:256] = odd
+        toep[d + 1, 128:256, 0:128] = odd
         return carry
 
     lax.fori_loop(0, NBLOCK, build, 0)
@@ -145,6 +148,8 @@
     send_out(om, bm, 3, m_rs)
     bm[chunk(me), :] = om[my_rows, my_lanes]
 
+    sub = lax.broadcasted_iota(jnp.int32, (BLOCK, BLOCK), 0)
+    col = lax.broadcasted_iota(jnp.int32, (BLOCK, BLOCK), 1)
     flip = (sub + col == BLOCK - 1).astype(BF16)
     gt_t[...] = dot(flip, rg[...], 1, 1).astype(BF16)
     arrived(sb.at[others], b_rs.at[0])
@@ -155,16 +160,16 @@
             prod[d] = dot(gt_t[:, 0:depth], rb[SHARE * d:SHARE * d + depth, :], 1, 0)
     prod[NBLOCK] = jnp.zeros((BLOCK, BLOCK), F32)
 
-    def lag_sums(plane, carry):
-        for e in range(2):
-            d = 2 * plane + e
-            both = jnp.where(col + sub >= BLOCK - 1, prod[d], prod[d + 1])
-            sums = jnp.sum(pltpu.roll(both, 1, 1, stride=1, stride_axis=0), axis=0, keepdims=True)
-            fa[RING * plane + 2 * e] = sums[:, 0:128]
-            fa[RING * plane + 2 * e + 1] = sums[:, 128:256]
+    def lag_sums(d, carry):
+        even = prod[d, 128:256, 0:128] + prod[d, 0:128, 128:256]
+        odd = prod[d, 128:256, 128:256] + prod[d + 1, 0:128, 0:128]
+        after = prod[d + 1, 128:256, 0:128] + prod[d + 1, 0:128, 128:256]
+        for e, (this, later) in enumerate(((even, odd), (odd, after))):
+            both = jnp.where(row + lane >= 127, this, later)
+            fa[2 * d + e] = jnp.sum(pltpu.roll(both, 1, 1, stride=1, stride_axis=0), axis=0, keepdims=True)
         return carry
 
-    lax.fori_loop(0, PLANES, lag_sums, 0)
+    lax.fori_loop(0, NBLOCK, lag_sums, 0)
 
     for dz in planes[:-1]:
         copy(fa.at[pl.ds(RING * zs[dz], RING)], ra.at[z], 5, a_rs.at[0], 0, dz, 0).start()
@@ -260,7 +265,7 @@
             pltpu.VMEM((width, rows), BF16),
             pltpu.VMEM((NFILT, 1, rows), F32),
             pltpu.VMEM((CTX, 1, rows), F32),
-            pltpu.VMEM((NBLOCK, BLOCK, BLOCK), BF16),
+            pltpu.VMEM((NBLOCK + 1, BLOCK, BLOCK), BF16),
             pltpu.VMEM((full, BLOCK), F32),
             pltpu.VMEM((BLOCK, full), BF16),
             pltpu.VMEM((NBLOCK + 1, BLOCK, BLOCK), F32),

time: 43.3 us -> 42.4 us (0.979)
  Pallas kernels: 42.6 us -> 41.6 us
    pallas_call x1, Pallas kernels: 41.5 us -> 40.6 us  [shards(): pl.pallas_call(functools.partial(kernel, nchan, scale), out_shape=(act, a...]
where the time goes in v4:
time: 42.4 us; the launch traced here: 42.3 us
  Pallas kernels  41.6 us (98%)
  between operations  0.64 us (2%)
    pallas_call x1, Pallas kernels, shards(): pl.pallas_call(functools.partial(kernel, nchan, scale), out_shape=(act, a...  40.6 us
    pallas_call x1, Pallas kernels, shards(): pl.pallas_call(store, out_shape=(act, act, act, act, jax.ShapeDtypeStruct...  1.01 us

profile of v4, /device:TPU:1, one launch (start us, length us, event | category | flops | bytes accessed | tf_op | source)
XLA Modules:
  0.0 42.3 jit_solution(17250811276763023934)
XLA Ops:
  0.6 40.6 %shard_map.92 = (bf16[128,1024]{1,0:T(8,128)(2,1)S(1)}, bf16[128,1024]{1,0:T(8,128)(2,1)S(1)}, bf16[128,1024]{1,0:T(8,128)(2,1)S(1)}, bf16[128,1024]{1,0:T(8,128)(2,1)S(1)}, f32[4,128]{1,0:T(4,128)S(1)}) custom-call(bf16[128,1024]{1,0:T(8,128)(2,1)} %q_hbm.1, bf16[128,1024]{1,0:T(8,128)(2,1)} %k_hbm.1, bf16[128,1024]{1,0:T(8,128)(2,1)} %v_hbm.1, ...), custom_call_target="tpu_custom_call" | custom-call | tf_op jit(solution)/shard_map/pallas_call | solution.py:246
  41.2 1.0 %shard_map.93 = (bf16[128,1024]{1,0:T(8,128)(2,1)}, bf16[128,1024]{1,0:T(8,128)(2,1)}, bf16[128,1024]{1,0:T(8,128)(2,1)}, bf16[128,1024]{1,0:T(8,128)(2,1)}, f32[4,128]{1,0:T(4,128)}) custom-call(bf16[128,1024]{1,0:T(8,128)(2,1)S(1)} %get-tuple-element.10.refs_0_, bf16[128,1024]{1,0:T(8,128)(2,1)S(1)} %get-tuple-element.11.refs_1_, ...), custom_call_target="tpu_custom_call" | custom-call | tf_op jit(solution)/shard_map/pallas_call | solution.py:281

commit v5 on v4

--- a/solution.py
+++ b/solution.py
@@ -29,7 +29,7 @@
            q_hbm, k_hbm, v_hbm, taps_hbm, c_hbm,
            out_ref, qg_ref, kg_ref, vg_ref, fg_ref,
            q_ref, k_ref, v_ref, taps_ref, c_ref, load_sem,
-           sg, sb, rg, rb, om, og, bm, bg, ts, tr, toep, acc, gt_t, prod, fa, ra, sbuf, rf,
+           sg, sb, rg, rb, om, og, bm, bg, ts, tr, toep, acc, gt_t, prod, fold, fa, ra, sbuf, rf,
            send_sem, t_rs, g_rs, b_rs, m_rs, o_rs, a_rs, f_rs):
     ch = lax.axis_index("chan")
     me = lax.axis_index("ctx")
@@ -100,8 +100,8 @@
         for dz, dy in peers:
             copy(send.at[chunk(zs[dz] * RING + ys[dy]), :], recv.at[my_rows, my_lanes], n, rs.at[0], 0, dz, dy).start()
 
-    def send_out(send, recv, n, rs):
-        for dz, dy in peers:
+    def send_out(send, recv, n, rs, which=peers):
+        for dz, dy in which:
             r, l = places[dz, dy]
             copy(send.at[r, l], recv.at[chunk(me), :], n, rs.at[(PLANES - dz) % PLANES], 0, dz, dy).start()
 
@@ -145,7 +145,8 @@
         else:
             acc[SHARE * d:full, :] += part
     om[...] = acc[...].astype(BF16)
-    send_out(om, bm, 3, m_rs)
+    held = planes[-3:]
+    send_out(om, bm, 3, m_rs, [peer for peer in peers if peer[0] not in held])
     bm[chunk(me), :] = om[my_rows, my_lanes]
 
     sub = lax.broadcasted_iota(jnp.int32, (BLOCK, BLOCK), 0)
@@ -153,27 +154,33 @@
     flip = (sub + col == BLOCK - 1).astype(BF16)
     gt_t[...] = dot(flip, rg[...], 1, 1).astype(BF16)
     arrived(sb.at[others], b_rs.at[0])
-    for group in range(NBLOCK // GROUPS):
-        depth = full - group * GROUPS * SHARE
-        for s in range(GROUPS):
-            d = group * GROUPS + s
-            prod[d] = dot(gt_t[:, 0:depth], rb[SHARE * d:SHARE * d + depth, :], 1, 0)
+    def product(d):
+        depth = full - d // GROUPS * GROUPS * SHARE
+        prod[d] = dot(gt_t[:, 0:depth], rb[SHARE * d:SHARE * d + depth, :], 1, 0)
+
+    def diagonals(e):
+        d = e // 2
+        if e % 2:
+            return prod[d, 128:256, 128:256] + prod[d + 1, 0:128, 0:128]
+        return prod[d, 128:256, 0:128] + prod[d, 0:128, 128:256]
+
     prod[NBLOCK] = jnp.zeros((BLOCK, BLOCK), F32)
-
-    def lag_sums(d, carry):
-        even = prod[d, 128:256, 0:128] + prod[d, 0:128, 128:256]
-        odd = prod[d, 128:256, 128:256] + prod[d + 1, 0:128, 0:128]
-        after = prod[d + 1, 128:256, 0:128] + prod[d + 1, 0:128, 128:256]
-        for e, (this, later) in enumerate(((even, odd), (odd, after))):
-            both = jnp.where(row + lane >= 127, this, later)
-            fa[2 * d + e] = jnp.sum(pltpu.roll(both, 1, 1, stride=1, stride_axis=0), axis=0, keepdims=True)
-        return carry
-
-    lax.fori_loop(0, NBLOCK, lag_sums, 0)
+    wide = row + lane >= 127
+    later = jnp.zeros((128, 128), F32)
+    for d in range(NBLOCK - 1, -1, -1):
+        product(d)
+        for e in (2 * d + 1, 2 * d):
+            this = diagonals(e)
+            both = pltpu.roll(jnp.where(wide, this, later), 1, 1, stride=1, stride_axis=0)
+            fold[e] = jnp.sum(both.reshape(16, 8, 128), axis=0)
+            later = this
+    for e in range(CTX):
+        fa[e] = jnp.sum(fold[e], axis=0, keepdims=True)
 
     for dz in planes[:-1]:
         copy(fa.at[pl.ds(RING * zs[dz], RING)], ra.at[z], 5, a_rs.at[0], 0, dz, 0).start()
     ra[z] = fa[pl.ds(RING * z, RING)]
+    send_out(om, bm, 3, m_rs, [peer for peer in peers if peer[0] in held])
 
     for d in range(NBLOCK):
         part = dot(rb[SHARE * d:full, :], toep[d], 1, 1)
@@ -269,6 +276,7 @@
             pltpu.VMEM((full, BLOCK), F32),
             pltpu.VMEM((BLOCK, full), BF16),
             pltpu.VMEM((NBLOCK + 1, BLOCK, BLOCK), F32),
+            pltpu.VMEM((CTX, 8, rows), F32),
             pltpu.VMEM((CTX, 1, rows), F32),
             pltpu.VMEM((PLANES, RING, 1, rows), F32),
             pltpu.VMEM((RING, 1, rows), F32),

time: 42.4 us -> 41.3 us (0.974)
  Pallas kernels: 41.6 us -> 40.6 us
    pallas_call x1, Pallas kernels: 40.6 us -> 39.6 us  [shards(): pl.pallas_call(functools.partial(kernel, nchan, scale), out_shape=(act, a...]
where the time goes in v5:
time: 41.3 us; the launch traced here: 41.2 us
  Pallas kernels  40.6 us (98%)
  between operations  0.64 us (2%)
    pallas_call x1, Pallas kernels, shards(): pl.pallas_call(functools.partial(kernel, nchan, scale), out_shape=(act, a...  39.6 us
    pallas_call x1, Pallas kernels, shards(): pl.pallas_call(store, out_shape=(act, act, act, act, jax.ShapeDtypeStruct...  1.01 us

profile of v5, /device:TPU:1, one launch (start us, length us, event | category | flops | bytes accessed | tf_op | source)
XLA Modules:
  0.0 41.2 jit_solution(1556786412953422994)
XLA Ops:
  0.6 39.6 %shard_map.92 = (bf16[128,1024]{1,0:T(8,128)(2,1)S(1)}, bf16[128,1024]{1,0:T(8,128)(2,1)S(1)}, bf16[128,1024]{1,0:T(8,128)(2,1)S(1)}, bf16[128,1024]{1,0:T(8,128)(2,1)S(1)}, f32[4,128]{1,0:T(4,128)S(1)}) custom-call(bf16[128,1024]{1,0:T(8,128)(2,1)} %q_hbm.1, bf16[128,1024]{1,0:T(8,128)(2,1)} %k_hbm.1, bf16[128,1024]{1,0:T(8,128)(2,1)} %v_hbm.1, ...), custom_call_target="tpu_custom_call" | custom-call | tf_op jit(solution)/shard_map/pallas_call | solution.py:253
  40.2 1.0 %shard_map.93 = (bf16[128,1024]{1,0:T(8,128)(2,1)}, bf16[128,1024]{1,0:T(8,128)(2,1)}, bf16[128,1024]{1,0:T(8,128)(2,1)}, bf16[128,1024]{1,0:T(8,128)(2,1)}, f32[4,128]{1,0:T(4,128)}) custom-call(bf16[128,1024]{1,0:T(8,128)(2,1)S(1)} %get-tuple-element.10.refs_0_, bf16[128,1024]{1,0:T(8,128)(2,1)S(1)} %get-tuple-element.11.refs_1_, ...), custom_call_target="tpu_custom_call" | custom-call | tf_op jit(solution)/shard_map/pallas_call | solution.py:289

commit v6 on v5

--- a/solution.py
+++ b/solution.py
@@ -40,7 +40,8 @@
     ps = [ch] + [lax.rem(ch + p, nchan) for p in range(1, nchan)]
     planes = (4, 3, 5, 2, 6, 1, 7, 0)
     peers = [(dz, dy) for dz in planes for dy in range(RING) if dz or dy]
-    near = [(p, dy) for p in range(nchan) for dy in range(RING) if p or dy]
+    far = sorted(range(nchan), key=lambda p: -min(p, nchan - p))
+    near = [(p, dy) for p in far for dy in (2, 1, 3, 0) if p or dy]
 
     barrier = pltpu.get_barrier_semaphore()
 
@@ -189,7 +190,8 @@
         else:
             acc[0:full - SHARE * d, :] += part
     og[...] = acc[...].astype(BF16)
-    send_out(og, bg, 4, o_rs)
+    kept = planes[-2:]
+    send_out(og, bg, 4, o_rs, [peer for peer in peers if peer[0] not in kept])
     bg[chunk(me), :] = og[my_rows, my_lanes]
 
     def tiles(recv, rs, fn):
@@ -215,6 +217,7 @@
         copy(sbuf.at[pl.ds(ys[dy], 1)], rf.at[pl.ds(ch * RING + y, 1)], 6, f_rs.at[0], p, 0, dy).start()
     rf[pl.ds(ch * RING + y, 1)] = sbuf[pl.ds(y, 1)]
 
+    send_out(og, bg, 4, o_rs, [peer for peer in peers if peer[0] in kept])
     tiles(bm, m_rs, finish_mixed)
     tiles(bg, o_rs, finish_grad)
 

time: 41.3 us -> 41.3 us (level)
  no operation moved by 1% of the time
where the time goes in v6:
time: 41.3 us; the launch traced here: 41.2 us
  Pallas kernels  40.5 us (98%)
  between operations  0.64 us (2%)
    pallas_call x1, Pallas kernels, shards(): pl.pallas_call(functools.partial(kernel, nchan, scale), out_shape=(act, a...  39.5 us
    pallas_call x1, Pallas kernels, shards(): pl.pallas_call(store, out_shape=(act, act, act, act, jax.ShapeDtypeStruct...  1.01 us

profile of v6, /device:TPU:1, one launch (start us, length us, event | category | flops | bytes accessed | tf_op | source)
XLA Modules:
  0.0 41.2 jit_solution(15444858851042222095)
XLA Ops:
  0.6 39.5 %shard_map.92 = (bf16[128,1024]{1,0:T(8,128)(2,1)S(1)}, bf16[128,1024]{1,0:T(8,128)(2,1)S(1)}, bf16[128,1024]{1,0:T(8,128)(2,1)S(1)}, bf16[128,1024]{1,0:T(8,128)(2,1)S(1)}, f32[4,128]{1,0:T(4,128)S(1)}) custom-call(bf16[128,1024]{1,0:T(8,128)(2,1)} %q_hbm.1, bf16[128,1024]{1,0:T(8,128)(2,1)} %k_hbm.1, bf16[128,1024]{1,0:T(8,128)(2,1)} %v_hbm.1, ...), custom_call_target="tpu_custom_call" | custom-call | tf_op jit(solution)/shard_map/pallas_call | solution.py:256
  40.1 1.0 %shard_map.93 = (bf16[128,1024]{1,0:T(8,128)(2,1)}, bf16[128,1024]{1,0:T(8,128)(2,1)}, bf16[128,1024]{1,0:T(8,128)(2,1)}, bf16[128,1024]{1,0:T(8,128)(2,1)}, f32[4,128]{1,0:T(4,128)}) custom-call(bf16[128,1024]{1,0:T(8,128)(2,1)S(1)} %get-tuple-element.10.refs_0_, bf16[128,1024]{1,0:T(8,128)(2,1)S(1)} %get-tuple-element.11.refs_1_, ...), custom_call_target="tpu_custom_call" | custom-call | tf_op jit(solution)/shard_map/pallas_call | solution.py:292
